TPU v7x, 32 devices: a whole 2x2x4 slice. The times are simulated.
32 devices in a mesh: shard: 4 (over y, x), ctx: 8 (over z, core).
Axes of the slice: x: 2, y: 2, z: 4, core: 2. Of those that a mesh axis runs over, the one named last changes fastest.
Arguments:
- tokens: bfloat16 [4, 1024, 768], P('shard', 'ctx'), may hold values from -60 to 60
- lengths: int32 [4], P('shard'), may hold values from 128 to 1024, as said below
- cotangent: bfloat16 [4, 1024, 768], P('shard', 'ctx'), may hold values from -6 to 6
- w_qkv: bfloat16 [768, 2304], P('shard'), may hold values from -0.21875 to 0.21875
- b_query: bfloat16 [768], P('shard'), may hold values from -3 to 3
- b_value: bfloat16 [768], P('shard'), may hold values from -3 to 3
- w_out: bfloat16 [768, 768], P('shard'), may hold values from -3.5 to 3.5
- b_out: bfloat16 [768], P('shard'), may hold values from -3 to 3
- ln1_gain: bfloat16 [768], P('shard'), may hold values from 0.25 to 1.75
- ln1_bias: bfloat16 [768], P('shard'), may hold values from -3 to 3
- w_up: bfloat16 [768, 3072], P('shard'), may hold values from -0.21875 to 0.21875
- b_up: bfloat16 [3072], P('shard'), may hold values from -3 to 3
- w_down: bfloat16 [3072, 768], P('shard'), may hold values from -0.109375 to 0.109375
- b_down: bfloat16 [768], P('shard'), may hold values from -3 to 3
- ln2_gain: bfloat16 [768], P('shard'), may hold values from 0.25 to 1.75
- ln2_bias: bfloat16 [768], P('shard'), may hold values from -3 to 3
Outputs:
- output: bfloat16 [4, 1024, 768], P('shard', 'ctx')
- tokens_grad: float32 [4, 1024, 768], P('shard', 'ctx')
- w_qkv_grad: float32 [768, 2304], P('shard')
- b_query_grad: float32 [768], P('shard')
- b_value_grad: float32 [768], P('shard')
- w_out_grad: float32 [768, 768], P('shard')
- b_out_grad: float32 [768], P('shard')
- ln1_gain_grad: float32 [768], P('shard')
- ln1_bias_grad: float32 [768], P('shard')
- w_up_grad: float32 [768, 3072], P('shard')
- b_up_grad: float32 [3072], P('shard')
- w_down_grad: float32 [3072, 768], P('shard')
- b_down_grad: float32 [768], P('shard')
- ln2_gain_grad: float32 [768], P('shard')
- ln2_bias_grad: float32 [768], P('shard')
Inputs may be any that keep to these rules, and one draw needn't show every extreme that they name: `lengths`: each sequence has at least one valid token; some sequence is entirely valid.
All inputs are finite; a program needn't handle non-finite values.
Results may differ from a plain program's by a relative error of at most 0.035.
The roundings to bfloat16 on the way count: a program that leaves them out, or rounds other values in their place, can miss the bound.
Values may be sent and summed in bfloat16 or wider, within the bound.
A program may use at most 128 MiB of HBM per device.

v0:
```python
import math
import jax
import jax.numpy as jnp
from jax import lax
from jax.sharding import PartitionSpec as P

HEADS = 12
EPS = 1e-06


def normalize(z):
    centre = z - jnp.mean(z, axis=-1, keepdims=True)
    rstd = lax.rsqrt(jnp.mean(centre * centre, axis=-1, keepdims=True) + EPS)
    return (centre * rstd, rstd)


def norm_back(dnorm, normed, rstd):
    return rstd * (
        dnorm
        - jnp.mean(dnorm, axis=-1, keepdims=True)
        - normed * jnp.mean(dnorm * normed, axis=-1, keepdims=True)
    )


def gelu_exact(t):
    return jax.nn.gelu(t, approximate=False)


def contract_dims(left, right, left_dim, right_dim):
    return lax.dot_general(
        left, right, (((left_dim,), (right_dim,)), ((), ())), preferred_element_type=jnp.float32
    )


def heads_first(a):
    return a.reshape(HEADS, a.shape[0] // HEADS, a.shape[1])


def local(
    tokens,
    lengths,
    cotangent,
    w_qkv,
    b_query,
    b_value,
    w_out,
    b_out,
    ln1_gain,
    ln1_bias,
    w_up,
    b_up,
    w_down,
    b_down,
    ln2_gain,
    ln2_bias,
):
    single_float = jnp.float32
    bf16 = jnp.bfloat16
    full = (
        lax.all_gather(w_qkv, "shard", axis=0, tiled=True),
        lax.all_gather(b_query, "shard", axis=0, tiled=True),
        lax.all_gather(b_value, "shard", axis=0, tiled=True),
        lax.all_gather(w_out, "shard", axis=0, tiled=True),
        lax.all_gather(b_out, "shard", axis=0, tiled=True),
        lax.all_gather(ln1_gain, "shard", axis=0, tiled=True),
        lax.all_gather(ln1_bias, "shard", axis=0, tiled=True),
        lax.all_gather(w_up, "shard", axis=0, tiled=True),
        lax.all_gather(b_up, "shard", axis=0, tiled=True),
        lax.all_gather(w_down, "shard", axis=0, tiled=True),
        lax.all_gather(b_down, "shard", axis=0, tiled=True),
        lax.all_gather(ln2_gain, "shard", axis=0, tiled=True),
        lax.all_gather(ln2_bias, "shard", axis=0, tiled=True),
    )
    wq_full, wo_full, wu_full, wd_full = (full[0], full[3], full[7], full[9])
    bq, bv, bo = (
        full[1].astype(single_float),
        full[2].astype(single_float),
        full[4].astype(single_float),
    )
    g1, c1, bu = (
        full[5].astype(single_float),
        full[6].astype(single_float),
        full[8].astype(single_float),
    )
    bd, g2, c2 = (
        full[10].astype(single_float),
        full[11].astype(single_float),
        full[12].astype(single_float),
    )
    x = tokens[0]
    width = x.shape[1]
    head_size = width // HEADS
    scale = 1.0 / math.sqrt(head_size)
    limit = lengths[0]
    qkv_t = contract_dims(wq_full, x, 0, 1)
    query_t = (qkv_t[:width] + bq[:, None]).astype(bf16)
    keys_t = qkv_t[width : 2 * width].astype(bf16)
    values_t = (qkv_t[2 * width :] + bv[:, None]).astype(bf16)
    all_keys, all_values = (
        lax.all_gather(keys_t, "ctx", axis=1, tiled=True),
        lax.all_gather(values_t, "ctx", axis=1, tiled=True),
    )
    total = all_keys.shape[1]
    valid = jnp.arange(total, dtype=jnp.int32) < limit

    def head_fwd(operations):
        query_index, key_index, value_index = operations
        scores = contract_dims(query_index, key_index, 0, 0) * scale
        scores = jnp.where(valid[None, :], scores, -1e30)
        peak = jnp.max(scores, axis=1, keepdims=True)
        lse = peak + jnp.log(jnp.sum(jnp.exp(scores - peak), axis=1, keepdims=True))
        probs = jnp.exp(scores - lse).astype(bf16)
        return (contract_dims(value_index, probs, 1, 1), lse[:, 0])

    ctx_heads, lse_all = lax.map(
        head_fwd, (heads_first(query_t), heads_first(all_keys), heads_first(all_values))
    )
    context_b_t = ctx_heads.reshape(width, -1).astype(bf16)
    z_one = x.astype(single_float) + contract_dims(context_b_t, wo_full, 0, 0) + bo
    n_one, rstd_one = normalize(z_one)
    x_one = n_one * g1 + c1
    x_one_b = x_one.astype(bf16)
    upper = jnp.dot(x_one_b, wu_full, preferred_element_type=single_float) + bu
    hidden_f, gelu_back = jax.vjp(gelu_exact, upper)
    hidden = hidden_f.astype(bf16)
    z_two = x_one + jnp.dot(hidden, wd_full, preferred_element_type=single_float) + bd
    n_two, rstd_two = normalize(z_two)
    out = (n_two * g2 + c2).astype(bf16)
    wq_back, wo_back, wu_back, wd_back = (wq_full, wo_full, wu_full, wd_full)
    keys_b, values_b = (all_keys, all_values)
    grad = cotangent[0].astype(single_float)
    dg_two = jnp.sum(grad * n_two, axis=0)
    db_two = jnp.sum(grad, axis=0)
    dz_two = norm_back(grad * g2, n_two, rstd_two)
    dz_two_b = dz_two.astype(bf16)
    dw_down = contract_dims(hidden, dz_two_b, 0, 0)
    db_down = jnp.sum(dz_two, axis=0)
    dhid = contract_dims(dz_two_b, wd_back, 1, 1)
    dupper = gelu_back(dhid)[0]
    dupper_b = dupper.astype(bf16)
    dw_up = contract_dims(x_one_b, dupper_b, 0, 0)
    db_up = jnp.sum(dupper, axis=0)
    dx_one = dz_two + contract_dims(dupper_b, wu_back, 1, 1)
    dg_one = jnp.sum(dx_one * n_one, axis=0)
    db_one = jnp.sum(dx_one, axis=0)
    dz_one = norm_back(dx_one * g1, n_one, rstd_one)
    dz_one_b = dz_one.astype(bf16)
    dw_out = contract_dims(context_b_t, dz_one_b, 1, 0)
    db_out = jnp.sum(dz_one, axis=0)
    dctx_t = contract_dims(wo_back, dz_one_b, 1, 1)
    dctx_b_t = dctx_t.astype(bf16)
    delta = jnp.sum(heads_first(dctx_t) * ctx_heads, axis=1)
    qh = heads_first(query_t)

    def head_bwd(operations):
        query_index, key_index, value_index, lse_index, context_grad_index, delta_index = operations
        scores = contract_dims(query_index, key_index, 0, 0) * scale
        scores = jnp.where(valid[None, :], scores, -1e30)
        prob = jnp.exp(scores - lse_index[:, None])
        block_probs = prob.astype(bf16)
        value_gradient = contract_dims(context_grad_index, block_probs, 1, 0)
        prob_gradient = contract_dims(context_grad_index, value_index, 0, 0)
        dscore = (prob * (prob_gradient - delta_index[:, None])).astype(bf16)
        query_gradient = contract_dims(key_index, dscore, 1, 1) * scale
        key_gradient = contract_dims(query_index, dscore, 1, 0) * scale
        return (query_gradient, key_gradient, value_gradient)

    dqh, dkh, dvh = lax.map(
        head_bwd,
        (qh, heads_first(keys_b), heads_first(values_b), lse_all, heads_first(dctx_b_t), delta),
    )
    key_grad_t, value_grad_t = (
        lax.psum_scatter(
            dkh.reshape(width, -1).astype(jnp.bfloat16), "ctx", scatter_dimension=1, tiled=True
        ).astype(jnp.float32),
        lax.psum_scatter(
            dvh.reshape(width, -1).astype(jnp.bfloat16), "ctx", scatter_dimension=1, tiled=True
        ).astype(jnp.float32),
    )
    query_grad_t = dqh.reshape(width, -1)
    dqkv_b_t = jnp.concatenate([query_grad_t, key_grad_t, value_grad_t], axis=0).astype(bf16)
    dw_qkv = contract_dims(x, dqkv_b_t, 0, 1)
    dx = dz_one + contract_dims(dqkv_b_t, wq_back, 0, 1)
    grads = (
        dw_qkv,
        jnp.sum(query_grad_t, axis=1),
        jnp.sum(value_grad_t, axis=1),
        dw_out,
        db_out,
        dg_one,
        db_one,
        dw_up,
        db_up,
        dw_down,
        db_down,
        dg_two,
        db_two,
    )
    pieces = (
        lax.psum_scatter(
            grads[0].astype(jnp.bfloat16), "shard", scatter_dimension=0, tiled=True
        ).astype(jnp.float32),
        lax.psum_scatter(
            grads[1].astype(jnp.bfloat16), "shard", scatter_dimension=0, tiled=True
        ).astype(jnp.float32),
        lax.psum_scatter(
            grads[2].astype(jnp.bfloat16), "shard", scatter_dimension=0, tiled=True
        ).astype(jnp.float32),
        lax.psum_scatter(
            grads[3].astype(jnp.bfloat16), "shard", scatter_dimension=0, tiled=True
        ).astype(jnp.float32),
        lax.psum_scatter(
            grads[4].astype(jnp.bfloat16), "shard", scatter_dimension=0, tiled=True
        ).astype(jnp.float32),
        lax.psum_scatter(
            grads[5].astype(jnp.bfloat16), "shard", scatter_dimension=0, tiled=True
        ).astype(jnp.float32),
        lax.psum_scatter(
            grads[6].astype(jnp.bfloat16), "shard", scatter_dimension=0, tiled=True
        ).astype(jnp.float32),
        lax.psum_scatter(
            grads[7].astype(jnp.bfloat16), "shard", scatter_dimension=0, tiled=True
        ).astype(jnp.float32),
        lax.psum_scatter(
            grads[8].astype(jnp.bfloat16), "shard", scatter_dimension=0, tiled=True
        ).astype(jnp.float32),
        lax.psum_scatter(
            grads[9].astype(jnp.bfloat16), "shard", scatter_dimension=0, tiled=True
        ).astype(jnp.float32),
        lax.psum_scatter(
            grads[10].astype(jnp.bfloat16), "shard", scatter_dimension=0, tiled=True
        ).astype(jnp.float32),
        lax.psum_scatter(
            grads[11].astype(jnp.bfloat16), "shard", scatter_dimension=0, tiled=True
        ).astype(jnp.float32),
        lax.psum_scatter(
            grads[12].astype(jnp.bfloat16), "shard", scatter_dimension=0, tiled=True
        ).astype(jnp.float32),
    )
    summed = (
        lax.psum(pieces[0].astype(jnp.bfloat16), "ctx").astype(jnp.float32),
        lax.psum(pieces[1].astype(jnp.bfloat16), "ctx").astype(jnp.float32),
        lax.psum(pieces[2].astype(jnp.bfloat16), "ctx").astype(jnp.float32),
        lax.psum(pieces[3].astype(jnp.bfloat16), "ctx").astype(jnp.float32),
        lax.psum(pieces[4].astype(jnp.bfloat16), "ctx").astype(jnp.float32),
        lax.psum(pieces[5].astype(jnp.bfloat16), "ctx").astype(jnp.float32),
        lax.psum(pieces[6].astype(jnp.bfloat16), "ctx").astype(jnp.float32),
        lax.psum(pieces[7].astype(jnp.bfloat16), "ctx").astype(jnp.float32),
        lax.psum(pieces[8].astype(jnp.bfloat16), "ctx").astype(jnp.float32),
        lax.psum(pieces[9].astype(jnp.bfloat16), "ctx").astype(jnp.float32),
        lax.psum(pieces[10].astype(jnp.bfloat16), "ctx").astype(jnp.float32),
        lax.psum(pieces[11].astype(jnp.bfloat16), "ctx").astype(jnp.float32),
        lax.psum(pieces[12].astype(jnp.bfloat16), "ctx").astype(jnp.float32),
    )
    return (
        out[None],
        dx[None],
        summed[0],
        summed[1],
        summed[2],
        summed[3],
        summed[4],
        summed[5],
        summed[6],
        summed[7],
        summed[8],
        summed[9],
        summed[10],
        summed[11],
        summed[12],
    )


def solution(mesh):
    in_specs = (
        P("shard", "ctx", None),
        P("shard"),
        P("shard", "ctx", None),
        P("shard", None),
        P("shard"),
        P("shard"),
        P("shard", None),
        P("shard"),
        P("shard"),
        P("shard"),
        P("shard", None),
        P("shard"),
        P("shard", None),
        P("shard"),
        P("shard"),
        P("shard"),
    )
    out_specs = (
        P("shard", "ctx", None),
        P("shard", "ctx", None),
        P("shard", None),
        P("shard"),
        P("shard"),
        P("shard", None),
        P("shard"),
        P("shard"),
        P("shard"),
        P("shard", None),
        P("shard"),
        P("shard", None),
        P("shard"),
        P("shard"),
        P("shard"),
    )
    return jax.shard_map(local, mesh=mesh, in_specs=in_specs, out_specs=out_specs, check_vma=False)
```

profile of v0, /device:TPU:0, one launch (start us, length us, event | category | flops | bytes accessed | tf_op | source)
XLA Modules:
  0.0 760.2 jit_solution(821553112586905481)
XLA Ops:
  15.8 18.3 %all-reduce.20 = (bf16[768]{0:T(1024)(128)(2,1)S(1)}, bf16[768]{0:T(1024)(128)(2,1)S(1)}, bf16[768]{0:T(1024)(128)(2,1)S(1)}, bf16[768]{0:T(1024)(128)(2,1)S(1)}...) all-reduce(bf16[768]{0:T(1024)(128)(2,1)S(1)} %dynamic-update-slice, ...), channel_id=1, replica_groups=mesh['shard'=4,'ctx'=8] {'shard'}, use_global_device_ids=true, to_apply=%add.1 | all-reduce | flops 5376 | bytes 21504
  34.1 25.7 %all-gather.8.cloned.1.call-done = bf16[768,2304]{1,0:T(8,128)(2,1)} async-done(((bf16[192,2304]{1,0:T(8,128)(2,1)}), bf16[768,2304]{1,0:T(8,128)(2,1)}) %all-gather.8.cloned.1.call-update) | async-done | bytes 3538960 | tf_op jit(solution)/shard_map/all_gather | solution.py:60
  59.8 3.1 fusion.71
  66.6 8.3 %all-gather = bf16[4,1,768]{2,1,0:T(2,128)(2,1)S(1)} all-gather(bf16[1,1,768]{2,1,0:T(2,128)(2,1)S(1)} %reshape.174), channel_id=1, replica_groups=mesh['shard'=4,'ctx'=8] {'shard'}, dimensions={0}, use_global_device_ids=true | all-gather | bytes 7680 | tf_op jit(solution)/shard_map/all_gather | solution.py:68
  74.9 16.2 %all-gather.10.cloned.1.call-done = bf16[768,1024]{1,0:T(8,128)(2,1)} async-done(((bf16[768,128]{1,0:T(8,128)(2,1)}), bf16[768,1024]{1,0:T(8,128)(2,1)}) %all-gather.10.cloned.1.call-update) | async-done | bytes 1572880 | tf_op jit(solution)/shard_map/all_gather | solution.py:101
  91.2 28.1 %all-gather.12.cloned.1.call-done = bf16[768,1024]{1,0:T(8,128)(2,1)} async-done(((bf16[768,128]{1,0:T(8,128)(2,1)}), bf16[768,1024]{1,0:T(8,128)(2,1)}) %all-gather.12.cloned.1.call-update) | async-done | bytes 1572880 | tf_op jit(solution)/shard_map/all_gather | solution.py:100
  119.3 55.8 %while.28 = (s32[]{:T(128)}, f32[12,64,128]{2,1,0:T(8,128)S(1)}, f32[12,128]{1,0:T(8,128)}, bf16[12,64,1024]{2,1,0:T(8,128)(2,1)}, bf16[12,64,128]{2,1,0:T(8,128...) while((s32[]{:T(128)}, f32[12,64,128]{2,1,0:T(8,128)S(1)}, ...), condition=%wide.region_3.4_spmd.clone, body=%wide.region_0.3_spmd.clone.sunk | while | flops 34472832 | bytes 1892965 | solution.py:115
  175.2 1.8 fusion.90
  177.2 28.8 %all-gather.16.cloned.1.call-done = bf16[768,3072]{1,0:T(8,128)(2,1)} async-done(((bf16[192,3072]{1,0:T(8,128)(2,1)}), bf16[768,3072]{1,0:T(8,128)(2,1)}) %all-gather.16.cloned.1.call-update) | async-done | bytes 4718608 | tf_op jit(solution)/shard_map/all_gather | solution.py:67
  206.0 7.6 %multiply_convert_fusion = (bf16[128,3072]{1,0:T(8,128)(2,1)S(1)}, f32[128,3072]{1,0:T(8,128)}) fusion(f32[3072]{0:T(1024)S(1)} %bitcast.162, bf16[768,3072]{1,0:T(8,128)(2,1)} %all-gather.16.cloned.1.call-done, f32[128,768]{1,0:T(8,128)S(1)} %get-tuple-element.303, f32[768]{0:T(1024)S(1)} %convert_element_type.209, f32[768]{0:T(1024)S(1)} %convert_element_type.208, ...), kind=kOutput, calls=%fused_computation.67 | convolution fusion | flops 630423552 | bytes 7490560 | tf_op jit(solution)/shard_map/dot_general | solution.py:123
  213.7 51.0 %all-gather.18.cloned.1.call-done = bf16[3072,768]{1,0:T(8,128)(2,1)} async-done(((bf16[768,768]{1,0:T(8,128)(2,1)}), bf16[3072,768]{1,0:T(8,128)(2,1)}) %all-gather.18.cloned.1.call-update) | async-done | bytes 4718608 | tf_op jit(solution)/shard_map/all_gather | solution.py:69
  264.7 3.4 fusion.91
  269.9 5.5 fusion.93
  275.4 2.4 multiply_reduce_fusion
  280.6 1.9 copy.38
  282.6 1.6 multiply_reduce_fusion.1
  284.2 1.7 copy.37
  286.0 87.0 %while.29 = (s32[]{:T(128)}, f32[12,64,128]{2,1,0:T(8,128)S(1)}, bf16[12,64,1024]{2,1,0:T(8,128)(2,1)}, bf16[12,64,1024]{2,1,0:T(8,128)(2,1)}, bf16[12,64,1024]{...) while((s32[]{:T(128)}, f32[12,64,128]{2,1,0:T(8,128)S(1)}, ...), condition=%wide.region_14.15_spmd.clone, body=%wide.region_13.14_spmd.clone.sunk | while | flops 84878336 | bytes 3385469 | solution.py:168
  290.6 1.5 fusion.147
  297.8 1.5 fusion.147
  305.1 1.5 fusion.147
  312.3 1.5 fusion.147
  319.6 1.5 fusion.147
  326.8 1.5 fusion.147
  334.1 1.5 fusion.147
  341.3 1.5 fusion.147
  355.8 1.5 fusion.147
  373.0 2.6 copy.40
  375.7 2.6 copy.42
  379.3 30.6 %reduce-scatter.19.cloned.1.call-done = bf16[128,768]{1,0:T(8,128)(2,1)} async-done(((bf16[1024,768]{1,0:T(8,128)(2,1)}), bf16[128,768]{1,0:T(8,128)(2,1)}) %reduce-scatter.19.cloned.1.call-update) | async-done | bytes 196624
  411.0 34.3 %reduce-scatter.21.cloned.1.call-done = bf16[128,768]{1,0:T(8,128)(2,1)} async-done(((bf16[1024,768]{1,0:T(8,128)(2,1)}), bf16[128,768]{1,0:T(8,128)(2,1)}) %reduce-scatter.21.cloned.1.call-update) | async-done | bytes 196624
  446.5 2.8 fusion.47
  449.3 5.8 copy.44
  457.6 3.7 convolution_convert_fusion.1
  461.3 3.6 convolution_convert_fusion
  465.0 35.7 %reduce-scatter.23.cloned.1.call-done = bf16[192,2304]{1,0:T(8,128)(2,1)} async-done(((bf16[768,2304]{1,0:T(8,128)(2,1)}), bf16[192,2304]{1,0:T(8,128)(2,1)}) %reduce-scatter.23.cloned.1.call-update) | async-done | bytes 884752
  500.7 2.3 copy.45
  503.0 29.7 %reduce-scatter.13.cloned.1.call-done = bf16[192,768]{1,0:T(8,128)(2,1)} async-done(((bf16[768,768]{1,0:T(8,128)(2,1)}), bf16[192,768]{1,0:T(8,128)(2,1)}) %reduce-scatter.13.cloned.1.call-update) | async-done | bytes 294928 | tf_op jit(solution)/shard_map/reduce_scatter | solution.py:209
  532.8 60.0 %reduce-scatter.15.cloned.1.call-done = bf16[192,3072]{1,0:T(8,128)(2,1)} async-done(((bf16[768,3072]{1,0:T(8,128)(2,1)}), bf16[192,3072]{1,0:T(8,128)(2,1)}) %reduce-scatter.15.cloned.1.call-update) | async-done | bytes 1179664 | tf_op jit(solution)/shard_map/reduce_scatter | solution.py:221
  592.8 59.8 %reduce-scatter.17.cloned.1.call-done = bf16[768,768]{1,0:T(8,128)(2,1)} async-done(((bf16[3072,768]{1,0:T(8,128)(2,1)}), bf16[768,768]{1,0:T(8,128)(2,1)}) %reduce-scatter.17.cloned.1.call-update) | async-done | bytes 1179664 | tf_op jit(solution)/shard_map/reduce_scatter | solution.py:227
  652.7 1.7 reduce_sum.194
  659.2 16.7 %all-reduce.19 = (bf16[768]{0:T(1024)(128)(2,1)}, bf16[768]{0:T(1024)(128)(2,1)}, bf16[768]{0:T(1024)(128)(2,1)}, bf16[768]{0:T(1024)(128)(2,1)}, bf16[768]{0:T(...) all-reduce(bf16[768]{0:T(1024)(128)(2,1)} %dynamic-update-slice.7, ...), channel_id=1, replica_groups=mesh['shard'=4,'ctx'=8] {'shard'}, use_global_device_ids=true, to_apply=%add.7 | all-reduce | flops 9984 | bytes 39936
  686.7 15.6 %all-reduce.17 = (bf16[192]{0:T(256)(128)(2,1)}, bf16[192]{0:T(256)(128)(2,1)}, bf16[192]{0:T(256)(128)(2,1)}, bf16[192]{0:T(256)(128)(2,1)}, bf16[192]{0:T(256)...) all-reduce(bf16[192]{0:T(256)(128)(2,1)} %dynamic-slice.9, ...), channel_id=1, replica_groups=mesh['shard'=4,'ctx'=8] {'ctx'}, use_global_device_ids=true, to_apply=%region_21.22 | all-reduce | flops 2304 | bytes 9216 | tf_op jit(solution)/shard_map/psum | solution.py:242
  713.1 1.8 fusion.69
  715.0 3.3 fusion.55
  718.3 28.3 %all-reduce.23.cloned.1.call-done = (bf16[192,2304]{0,1:T(8,128)(2,1)}, bf16[192,768]{1,0:T(8,128)(2,1)}, bf16[192,3072]{1,0:T(8,128)(2,1)}, bf16[768,768]{1,0:T(8,128)(2,1)}) async-done(((bf16[192,2304]{0,1:T(8,128)(2,1)}, bf16[192,768]{1,0:T(8,128)(2,1)}, bf16[192,3072]{1,0:T(8,128)(2,1)}, bf16[768,768]{1,0:T(8,128)(2,1)}), (bf16[192,2304]{0,1:T(8,128)(2,1)}, bf16[192,768]{1,0:T(8,128)(2,1)}, ...) | async-done | bytes 3538960 | tf_op jit(solution)/shard_map/psum | solution.py:241
  746.6 3.0 convert_element_type.243
  749.7 1.6 convert_element_type.247
  (301 shorter events, 178.0 us)
Async XLA Ops:
  7.2 52.7 %all-gather.8.cloned.1.call-start = ((), (), s32[]{:S(2)}) async-start(), calls=%async_computation.6 | async-start | bytes 4423680 | tf_op jit(solution)/shard_map/all_gather | solution.py:60
  7.9 83.3 %all-gather.10.cloned.1.call-start = ((), (), s32[]{:S(2)}) async-start(), calls=%async_computation.7 | async-start | bytes 1769472 | tf_op jit(solution)/shard_map/all_gather | solution.py:101
  63.9 2.6 copy-start.22
  63.9 55.3 %all-gather.12.cloned.1.call-start = ((), (), s32[]{:S(2)}) async-start(), calls=%async_computation.8 | async-start | bytes 1769472 | tf_op jit(solution)/shard_map/all_gather | solution.py:100
  64.7 110.5 %all-gather.14.cloned.1.call-start = ((), (), s32[]{:S(2)}) async-start(), calls=%async_computation.9 | async-start | bytes 1474560 | tf_op jit(solution)/shard_map/all_gather | solution.py:63
  65.3 140.8 %all-gather.16.cloned.1.call-start = ((), (), s32[]{:S(2)}) async-start(), calls=%async_computation.10 | async-start | bytes 5898240 | tf_op jit(solution)/shard_map/all_gather | solution.py:67
  65.9 198.8 %all-gather.18.cloned.1.call-start = ((), (), s32[]{:S(2)}) async-start(), calls=%async_computation.11 | async-start | bytes 5898240 | tf_op jit(solution)/shard_map/all_gather | solution.py:69
  66.5 343.5 %reduce-scatter.19.cloned.1.call-start = ((), (), s32[]{:S(2)}) async-start(), calls=%async_computation.15 | async-start | bytes 1769472
  119.3 55.9 %copy-start.5 = (bf16[1,128,768]{2,1,0:T(8,128)(2,1)S(1)}, bf16[1,128,768]{2,1,0:T(8,128)(2,1)}, u32[]{:S(2)}) copy-start(bf16[1,128,768]{2,1,0:T(8,128)(2,1)} %param.20) | copy-start | bytes 589828
  175.2 38.5 %copy-start.9 = (bf16[12,64,128]{2,1,0:T(8,128)(2,1)}, bf16[12,64,128]{2,1,0:T(8,128)(2,1)S(1)}, u32[]{:S(2)}) copy-start(bf16[12,64,128]{2,1,0:T(8,128)(2,1)S(1)} %convert_element_type.205) | copy-start | bytes 589828
  177.2 98.2 %copy-start.16 = (f32[128]{0:T(128)}, f32[128]{0:T(128)S(1)}, u32[]{:S(2)}) copy-start(f32[128]{0:T(128)S(1)} %add_rsqrt_fusion.1) | copy-start | bytes 1540
  264.7 3.6 copy-start.11
  264.7 5.2 copy-start.3
  268.1 1.1 copy-start.1
  268.1 1.8 copy-start.23
  268.1 7.3 copy-start.18
  268.3 7.1 copy-start.21
  269.1 6.3 slice-start
  269.9 5.5 slice-start.1
  277.8 1.5 copy-start.4
  279.3 175.9 %copy-start.2 = (f32[128,768]{1,0:T(8,128)}, f32[128,768]{1,0:T(8,128)S(1)}, u32[]{:S(2)}) copy-start(f32[128,768]{1,0:T(8,128)S(1)} %get-tuple-element.291) | copy-start | bytes 1179652
  375.6 69.7 %reduce-scatter.21.cloned.1.call-start = ((), (), s32[]{:S(2)}) async-start(), calls=%async_computation.16 | async-start | bytes 1769472
  378.3 122.4 %reduce-scatter.23.cloned.1.call-start = ((), (), s32[]{:S(2)}) async-start(), calls=%async_computation.17 | async-start | bytes 4423680
  379.3 70.0 %copy-start.8 = (bf16[12,64,128]{2,1,0:T(8,128)(2,1)}, bf16[12,64,128]{2,1,0:T(8,128)(2,1)S(1)}, u32[]{:S(2)}) copy-start(bf16[12,64,128]{2,1,0:T(8,128)(2,1)S(1)} %get-tuple-element.298) | copy-start | bytes 589828
  411.0 38.3 %copy-start.6 = (bf16[768,128]{1,0:T(8,128)(2,1)}, bf16[768,128]{1,0:T(8,128)(2,1)S(1)}, u32[]{:S(2)}) copy-start(bf16[768,128]{1,0:T(8,128)(2,1)S(1)} %copy.41) | copy-start | bytes 589828
  446.4 2.9 copy-start.7
  455.1 0.9 copy-start.10
  455.1 2.4 copy-start.17
  455.1 77.6 %reduce-scatter.13.cloned.1.call-start = ((), (), s32[]{:S(2)}) async-start(), calls=%async_computation.12 | async-start | bytes 1474560 | tf_op jit(solution)/shard_map/reduce_scatter | solution.py:209
  457.5 135.3 %reduce-scatter.15.cloned.1.call-start = ((), (), s32[]{:S(2)}) async-start(), calls=%async_computation.13 | async-start | bytes 5898240 | tf_op jit(solution)/shard_map/reduce_scatter | solution.py:221
  461.3 191.4 %reduce-scatter.17.cloned.1.call-start = ((), (), s32[]{:S(2)}) async-start(), calls=%async_computation.14 | async-start | bytes 5898240 | tf_op jit(solution)/shard_map/reduce_scatter | solution.py:227
  464.9 281.7 %all-reduce.23.cloned.1.call-start = ((), (), s32[]{:S(2)}) async-start(), calls=%async_computation.18 | async-start | bytes 7667712 | tf_op jit(solution)/shard_map/psum | solution.py:241
  652.6 5.0 copy-start.15
  652.6 6.6 copy-start.20
  652.6 60.5 %copy-start.19 = (f32[128]{0:T(128)S(1)}, f32[128]{0:T(128)}, u32[]{:S(2)}) copy-start(f32[128]{0:T(128)} %copy-done.18) | copy-start | bytes 1540
  652.6 62.3 %copy-start = (bf16[768,2304]{1,0:T(8,128)(2,1)S(1)}, bf16[768,2304]{1,0:T(8,128)(2,1)}, u32[]{:S(2)}) copy-start(bf16[768,2304]{1,0:T(8,128)(2,1)} %all-gather.8.cloned.1.call-done) | copy-start | bytes 10616836
  746.6 3.0 copy-start.12
  749.7 1.7 copy-start.13
  751.2 1.6 copy-start.14
Sparse Core Ops, SparseCore 0:
  9.8 49.9 all-gather.7
  64.0 27.0 all-gather.9
  93.3 25.8 all-gather.11
  121.0 26.3 all-gather.13
  149.1 56.9 all-gather.15
  207.7 56.9 all-gather.17
  375.7 34.1 reduce-scatter.18
  412.8 32.5 reduce-scatter.20
  455.2 45.4 reduce-scatter.22
  504.1 28.6 reduce-scatter.12
  535.8 56.9 reduce-scatter.14
  595.6 56.9 reduce-scatter.16
  655.8 90.7 all-reduce.22
where the time goes:
time: 764 us; the launch traced here: 760 us
  waiting for transfers between devices  431 us (56%)
  matrix products  140 us (18%)
  local copies, waits for them, and re-layouts  66.7 us (9%)
  blocking collectives  58.9 us (8%)
  other arithmetic  46.2 us (6%)
  between operations  16.2 us (2%)
    dot_general x94, matrix products, contract_dims(): lax.dot_general(left, right, (((left_dim,), (right_dim,)), ((), ())), pre...  129 us
    unnamed x16, waiting for transfers between devices  103 us
    reduce_scatter x1, waiting for transfers between devices, local(): lax.psum_scatter(grads[7].astype(jnp.bfloat16), 'shard', scatter_dimensio...  60 us
    reduce_scatter x1, waiting for transfers between devices, local(): lax.psum_scatter(grads[9].astype(jnp.bfloat16), 'shard', scatter_dimensio...  59.8 us
    all_gather x1, waiting for transfers between devices, local(): lax.all_gather(w_down, 'shard', axis=0, tiled=True)  51 us
    unnamed x86, local copies, waits for them, and re-layouts  37.9 us
    unnamed x2, blocking collectives  35 us
    reduce_scatter x1, waiting for transfers between devices, local(): lax.psum_scatter(grads[3].astype(jnp.bfloat16), 'shard', scatter_dimensio...  29.7 us
  transfers between devices with their start and end apart: 13, of which 12 were waited for; matrix products, arithmetic and copies ran while one was open for 16% of the time, Pallas kernels for 0%

commit v1 on v0

--- a/solution.py
+++ b/solution.py
@@ -6,6 +6,23 @@
 
 HEADS = 12
 EPS = 1e-06
+
+
+def joined_along(parts, dim):
+    parts = jnp.moveaxis(parts, 0, dim)
+    shape = parts.shape
+    return parts.reshape(*shape[:dim], shape[dim] * shape[dim + 1], *shape[dim + 2 :])
+
+
+def gather_around(shard, axis, dim):
+    peers = lax.axis_size(axis)
+    forward = [(i, (i + 1) % peers) for i in range(peers)]
+    blocks = [shard]
+    while len(blocks) < peers:
+        blocks.append(lax.ppermute(blocks[-1], axis, forward))
+    mine = lax.axis_index(axis)
+    blocks = jnp.stack(blocks)[(mine - jnp.arange(peers)) % peers]
+    return joined_along(blocks, dim)
 
 
 def normalize(z):
@@ -66,7 +83,7 @@
         lax.all_gather(ln1_bias, "shard", axis=0, tiled=True),
         lax.all_gather(w_up, "shard", axis=0, tiled=True),
         lax.all_gather(b_up, "shard", axis=0, tiled=True),
-        lax.all_gather(w_down, "shard", axis=0, tiled=True),
+        gather_around(w_down, "shard", 0),
         lax.all_gather(b_down, "shard", axis=0, tiled=True),
         lax.all_gather(ln2_gain, "shard", axis=0, tiled=True),
         lax.all_gather(ln2_bias, "shard", axis=0, tiled=True),

time: 764 us -> 738 us (0.966)
  waiting for transfers between devices: 431 us -> 359 us
  blocking collectives: 58.9 us -> 80.9 us
    ppermute x0 -> x3, waiting for transfers between devices: none -> 53.9 us  [gather_around(): blocks.append(lax.ppermute(blocks[-1], axis, forward))]
    all_gather x1 -> x0, waiting for transfers between devices: 51 us -> none  [local(): lax.all_gather(w_down, 'shard', axis=0, tiled=True)]
    all_gather x1, waiting for transfers between devices: 28.8 us -> 0.43 us  [local(): lax.all_gather(w_up, 'shard', axis=0, tiled=True)]
    all_gather x1, waiting for transfers between devices: 28.1 us -> 0.01 us  [local(): lax.all_gather(keys_t, 'ctx', axis=1, tiled=True)]
    all_gather x1, blocking collectives: 8.3 us -> 29.7 us  [local(): lax.all_gather(b_up, 'shard', axis=0, tiled=True)]
    all_gather x1, waiting for transfers between devices: 16.2 us -> 0.01 us  [local(): lax.all_gather(values_t, 'ctx', axis=1, tiled=True)]
    dot_general x94, matrix products: 129 us -> 139 us  [contract_dims(): lax.dot_general(left, right, (((left_dim,), (right_dim,)), ((), ())), pre...]
    unnamed x16 -> x15, waiting for transfers between devices: 103 us -> 102 us
  transfers between devices with their start and end apart: 13 -> 15, of which waited for: 12 -> 11; matrix products, arithmetic and copies ran while one was open for 16% -> 17% of each run, Pallas kernels for 0% -> 0%
where the time goes in v1:
time: 738 us; the launch traced here: 730 us
  waiting for transfers between devices  359 us (49%)
  matrix products  146 us (20%)
  blocking collectives  80.9 us (11%)
  local copies, waits for them, and re-layouts  73.3 us (10%)
  other arithmetic  51.3 us (7%)
  between operations  16.5 us (2%)
    dot_general x94, matrix products, contract_dims(): lax.dot_general(left, right, (((left_dim,), (right_dim,)), ((), ())), pre...  139 us
    unnamed x15, waiting for transfers between devices  102 us
    reduce_scatter x1, waiting for transfers between devices, local(): lax.psum_scatter(grads[9].astype(jnp.bfloat16), 'shard', scatter_dimensio...  60 us
    reduce_scatter x1, waiting for transfers between devices, local(): lax.psum_scatter(grads[7].astype(jnp.bfloat16), 'shard', scatter_dimensio...  59.9 us
    ppermute x3, waiting for transfers between devices, gather_around(): blocks.append(lax.ppermute(blocks[-1], axis, forward))  53.9 us
    unnamed x82, local copies, waits for them, and re-layouts  39.1 us
    unnamed x2, blocking collectives  35.6 us
    reduce_scatter x1, waiting for transfers between devices, local(): lax.psum_scatter(grads[3].astype(jnp.bfloat16), 'shard', scatter_dimensio...  29.9 us
  transfers between devices with their start and end apart: 15, of which 11 were waited for; matrix products, arithmetic and copies ran while one was open for 17% of the time, Pallas kernels for 0%

profile of v1, /device:TPU:0, one launch (start us, length us, event | category | flops | bytes accessed | tf_op | source)
XLA Modules:
  0.0 730.1 jit_solution(4998123526281980113)
XLA Ops:
  15.8 18.9 %all-reduce.20 = (bf16[768]{0:T(1024)(128)(2,1)S(1)}, bf16[768]{0:T(1024)(128)(2,1)S(1)}, bf16[768]{0:T(1024)(128)(2,1)S(1)}, bf16[768]{0:T(1024)(128)(2,1)S(1)}...) all-reduce(bf16[768]{0:T(1024)(128)(2,1)S(1)} %dynamic-update-slice, ...), channel_id=1, replica_groups=mesh['shard'=4,'ctx'=8] {'shard'}, use_global_device_ids=true, to_apply=%add.1 | all-reduce | flops 5376 | bytes 21504
  34.7 25.1 %all-gather.7.cloned.1.call-done = bf16[768,2304]{1,0:T(8,128)(2,1)} async-done(((bf16[192,2304]{1,0:T(8,128)(2,1)}), bf16[768,2304]{1,0:T(8,128)(2,1)}) %all-gather.7.cloned.1.call-update) | async-done | bytes 3538960 | tf_op jit(solution)/shard_map/all_gather | solution.py:77
  59.8 3.1 fusion.71
  66.4 27.0 %collective-permute-done = bf16[768,768]{1,0:T(8,128)(2,1)S(1)} collective-permute-done((bf16[768,768]{1,0:T(8,128)(2,1)S(1)}, bf16[768,768]{1,0:T(8,128)(2,1)S(1)}, u32[]{:S(2)}, u32[]{:S(2)}) %collective-permute-start) | collective-permute-done | bytes 1179680 | tf_op jit(solution)/shard_map/ppermute | solution.py:22
  94.0 26.9 %collective-permute-done.1 = bf16[768,768]{1,0:T(8,128)(2,1)S(1)} collective-permute-done((bf16[768,768]{1,0:T(8,128)(2,1)S(1)}, bf16[768,768]{1,0:T(8,128)(2,1)S(1)}, u32[]{:S(2)}, u32[]{:S(2)}) %collective-permute-start.1) | collective-permute-done | bytes 1179680 | tf_op jit(solution)/shard_map/ppermute | solution.py:22
  122.3 29.7 %all-gather = bf16[4,1,768]{2,1,0:T(2,128)(2,1)S(1)} all-gather(bf16[1,1,768]{2,1,0:T(2,128)(2,1)S(1)} %reshape.235), channel_id=1, replica_groups=mesh['shard'=4,'ctx'=8] {'shard'}, dimensions={0}, use_global_device_ids=true | all-gather | bytes 7680 | tf_op jit(solution)/shard_map/all_gather | solution.py:85
  154.0 3.6 pad_maximum_fusion
  157.5 5.5 gather_fusion
  163.1 56.0 %while.28 = (s32[]{:T(128)}, f32[12,64,128]{2,1,0:T(8,128)S(1)}, f32[12,128]{1,0:T(8,128)}, bf16[12,64,1024]{2,1,0:T(8,128)(2,1)}, bf16[12,64,128]{2,1,0:T(8,128...) while((s32[]{:T(128)}, f32[12,64,128]{2,1,0:T(8,128)S(1)}, ...), condition=%wide.region_3.4_spmd.clone, body=%wide.region_0.3_spmd.clone.sunk | while | flops 34472832 | bytes 1892965 | solution.py:132
  219.2 1.8 fusion.92
  221.6 6.0 multiply_convert_fusion
  230.4 5.5 fusion.95
  235.9 2.3 multiply_reduce_fusion
  240.8 1.9 copy.38
  243.8 1.7 copy.37
  245.6 95.7 %while.29 = (s32[]{:T(128)}, f32[12,64,128]{2,1,0:T(8,128)S(1)}, bf16[12,64,1024]{2,1,0:T(8,128)(2,1)}, bf16[12,64,1024]{2,1,0:T(8,128)(2,1)}, bf16[12,64,1024]{...) while((s32[]{:T(128)}, f32[12,64,128]{2,1,0:T(8,128)S(1)}, ...), condition=%wide.region_14.15_spmd.clone, body=%wide.region_13.14_spmd.clone.sunk | while | flops 84878336 | bytes 3385469 | solution.py:185
  249.3 1.6 fusion.148
  257.3 1.6 fusion.148
  265.3 1.6 fusion.148
  273.2 1.6 fusion.148
  281.2 1.6 fusion.148
  289.2 1.6 fusion.148
  297.2 1.6 fusion.148
  305.1 1.6 fusion.148
  313.1 1.6 fusion.148
  321.1 1.6 fusion.148
  329.1 1.6 fusion.148
  341.3 2.6 copy.40
  344.0 2.6 copy.42
  347.4 30.9 %reduce-scatter.19.cloned.1.call-done = bf16[128,768]{1,0:T(8,128)(2,1)} async-done(((bf16[1024,768]{1,0:T(8,128)(2,1)}), bf16[128,768]{1,0:T(8,128)(2,1)}) %reduce-scatter.19.cloned.1.call-update) | async-done | bytes 196624
  379.4 34.4 %reduce-scatter.21.cloned.1.call-done = bf16[128,768]{1,0:T(8,128)(2,1)} async-done(((bf16[1024,768]{1,0:T(8,128)(2,1)}), bf16[128,768]{1,0:T(8,128)(2,1)}) %reduce-scatter.21.cloned.1.call-update) | async-done | bytes 196624
  414.9 3.8 fusion.47
  418.7 5.8 copy.44
  427.2 3.6 convolution_convert_fusion.1
  430.9 3.6 convolution_convert_fusion
  434.6 35.6 %reduce-scatter.23.cloned.1.call-done = bf16[192,2304]{1,0:T(8,128)(2,1)} async-done(((bf16[768,2304]{1,0:T(8,128)(2,1)}), bf16[192,2304]{1,0:T(8,128)(2,1)}) %reduce-scatter.23.cloned.1.call-update) | async-done | bytes 884752
  470.2 2.3 copy.45
  472.5 29.9 %reduce-scatter.13.cloned.1.call-done = bf16[192,768]{1,0:T(8,128)(2,1)} async-done(((bf16[768,768]{1,0:T(8,128)(2,1)}), bf16[192,768]{1,0:T(8,128)(2,1)}) %reduce-scatter.13.cloned.1.call-update) | async-done | bytes 294928 | tf_op jit(solution)/shard_map/reduce_scatter | solution.py:226
  502.5 59.9 %reduce-scatter.15.cloned.1.call-done = bf16[192,3072]{1,0:T(8,128)(2,1)} async-done(((bf16[768,3072]{1,0:T(8,128)(2,1)}), bf16[192,3072]{1,0:T(8,128)(2,1)}) %reduce-scatter.15.cloned.1.call-update) | async-done | bytes 1179664 | tf_op jit(solution)/shard_map/reduce_scatter | solution.py:238
  562.3 60.0 %reduce-scatter.17.cloned.1.call-done = bf16[768,768]{1,0:T(8,128)(2,1)} async-done(((bf16[3072,768]{1,0:T(8,128)(2,1)}), bf16[768,768]{1,0:T(8,128)(2,1)}) %reduce-scatter.17.cloned.1.call-update) | async-done | bytes 1179664 | tf_op jit(solution)/shard_map/reduce_scatter | solution.py:244
  622.3 1.7 reduce_sum.194
  628.9 16.7 %all-reduce.19 = (bf16[768]{0:T(1024)(128)(2,1)}, bf16[768]{0:T(1024)(128)(2,1)}, bf16[768]{0:T(1024)(128)(2,1)}, bf16[768]{0:T(1024)(128)(2,1)}, bf16[768]{0:T(...) all-reduce(bf16[768]{0:T(1024)(128)(2,1)} %dynamic-update-slice.7, ...), channel_id=1, replica_groups=mesh['shard'=4,'ctx'=8] {'shard'}, use_global_device_ids=true, to_apply=%add.7 | all-reduce | flops 9984 | bytes 39936
  656.4 15.6 %all-reduce.17 = (bf16[192]{0:T(256)(128)(2,1)}, bf16[192]{0:T(256)(128)(2,1)}, bf16[192]{0:T(256)(128)(2,1)}, bf16[192]{0:T(256)(128)(2,1)}, bf16[192]{0:T(256)...) all-reduce(bf16[192]{0:T(256)(128)(2,1)} %dynamic-slice.9, ...), channel_id=1, replica_groups=mesh['shard'=4,'ctx'=8] {'ctx'}, use_global_device_ids=true, to_apply=%region_21.22 | all-reduce | flops 2304 | bytes 9216 | tf_op jit(solution)/shard_map/psum | solution.py:259
  683.1 1.8 fusion.69
  684.9 3.3 fusion.55
  688.2 28.0 %all-reduce.23.cloned.1.call-done = (bf16[192,2304]{0,1:T(8,128)(2,1)}, bf16[192,768]{1,0:T(8,128)(2,1)}, bf16[192,3072]{1,0:T(8,128)(2,1)}, bf16[768,768]{1,0:T(8,128)(2,1)}) async-done(((bf16[192,2304]{0,1:T(8,128)(2,1)}, bf16[192,768]{1,0:T(8,128)(2,1)}, bf16[192,3072]{1,0:T(8,128)(2,1)}, bf16[768,768]{1,0:T(8,128)(2,1)}), (bf16[192,2304]{0,1:T(8,128)(2,1)}, bf16[192,768]{1,0:T(8,128)(2,1)}, ...) | async-done | bytes 3538960 | tf_op jit(solution)/shard_map/psum | solution.py:258
  716.2 3.0 convert_element_type.243
  719.2 1.6 convert_element_type.247
  (305 shorter events, 189.8 us)
Async XLA Ops:
  7.2 52.7 %all-gather.7.cloned.1.call-start = ((), (), s32[]{:S(2)}) async-start(), calls=%async_computation.6 | async-start | bytes 4423680 | tf_op jit(solution)/shard_map/all_gather | solution.py:77
  7.9 155.1 %all-gather.9.cloned.1.call-start = ((), (), s32[]{:S(2)}) async-start(), calls=%async_computation.7 | async-start | bytes 1769472 | tf_op jit(solution)/shard_map/all_gather | solution.py:118
  63.0 1.9 copy-start.10
  64.0 99.0 %all-gather.11.cloned.1.call-start = ((), (), s32[]{:S(2)}) async-start(), calls=%async_computation.8 | async-start | bytes 1769472 | tf_op jit(solution)/shard_map/all_gather | solution.py:117
  64.8 154.4 %all-gather.13.cloned.1.call-start = ((), (), s32[]{:S(2)}) async-start(), calls=%async_computation.9 | async-start | bytes 1474560 | tf_op jit(solution)/shard_map/all_gather | solution.py:80
  64.9 28.5 %collective-permute-start = (bf16[768,768]{1,0:T(8,128)(2,1)S(1)}, bf16[768,768]{1,0:T(8,128)(2,1)S(1)}, u32[]{:S(2)}, u32[]{:S(2)}) collective-permute-start(bf16[768,768]{1,0:T(8,128)(2,1)S(1)} %copy-done.10), channel_id=1, source_target_pairs={{0,8},{8,16},{16,24},{24,0},{1,9},{9,17},{17,25},{25,1},{2,10},{10... | collective-permute-start | bytes 3538952 | tf_op jit(solution)/shard_map/ppermute | solution.py:22
  93.3 27.6 %collective-permute-start.1 = (bf16[768,768]{1,0:T(8,128)(2,1)S(1)}, bf16[768,768]{1,0:T(8,128)(2,1)S(1)}, u32[]{:S(2)}, u32[]{:S(2)}) collective-permute-start(bf16[768,768]{1,0:T(8,128)(2,1)S(1)} %collective-permute-done), channel_id=1, source_target_pairs={{0,8},{8,16},{16,24},{24,0},{1,9},{9,17},{17,25},{25,1},{2,10},{10... | collective-permute-start | bytes 3538952 | tf_op jit(solution)/shard_map/ppermute | solution.py:22
  93.9 127.7 %all-gather.15.cloned.1.call-start = ((), (), s32[]{:S(2)}) async-start(), calls=%async_computation.10 | async-start | bytes 5898240 | tf_op jit(solution)/shard_map/all_gather | solution.py:84
  120.9 33.0 %collective-permute-start.2 = (bf16[768,768]{1,0:T(8,128)(2,1)S(1)}, bf16[768,768]{1,0:T(8,128)(2,1)}, u32[]{:S(2)}, u32[]{:S(2)}) collective-permute-start(bf16[768,768]{1,0:T(8,128)(2,1)S(1)} %collective-permute-done.1), channel_id=1, source_target_pairs={{0,8},{8,16},{16,24},{24,0},{1,9},{9,17},{17,25},{25,1},{2,10},{10... | collective-permute-start | bytes 3538952 | tf_op jit(solution)/shard_map/ppermute | solution.py:22
  121.0 257.4 %reduce-scatter.19.cloned.1.call-start = ((), (), s32[]{:S(2)}) async-start(), calls=%async_computation.14 | async-start | bytes 1769472
  163.1 56.1 %copy-start.4 = (bf16[1,128,768]{2,1,0:T(8,128)(2,1)S(1)}, bf16[1,128,768]{2,1,0:T(8,128)(2,1)}, u32[]{:S(2)}) copy-start(bf16[1,128,768]{2,1,0:T(8,128)(2,1)} %param.20) | copy-start | bytes 589828
  163.1 56.1 %copy-start.14 = (f32[768]{0:T(1024)S(1)}, f32[768]{0:T(1024)}, u32[]{:S(2)}) copy-start(f32[768]{0:T(1024)} %convert_element_type.207) | copy-start | bytes 9220
  219.1 2.5 copy-start.15
  219.1 8.5 %copy-start.7 = (bf16[12,64,128]{2,1,0:T(8,128)(2,1)}, bf16[12,64,128]{2,1,0:T(8,128)(2,1)S(1)}, u32[]{:S(2)}) copy-start(bf16[12,64,128]{2,1,0:T(8,128)(2,1)S(1)} %convert_element_type.205) | copy-start | bytes 589828
  219.2 8.4 %slice-start = ((s8[4718592]{0:T(1024)(128)(4,1)}), s8[524288]{0:T(1024)(128)(4,1)S(1)}, s32[]{:S(2)}) async-start(s8[4718592]{0:T(1024)(128)(4,1)} %bitcast.151), calls=%async_computation.18 | async-start | bytes 1048576
  221.6 6.0 slice-start.1
  227.7 1.1 copy-start.9
  228.6 1.0 copy-start.1
  228.6 7.3 copy-start.16
  228.8 7.0 copy-start.19
  229.6 6.3 slice-start.2
  230.4 5.5 slice-start.3
  238.2 1.3 copy-start.3
  239.0 185.6 %copy-start.2 = (f32[128,768]{1,0:T(8,128)}, f32[128,768]{1,0:T(8,128)S(1)}, u32[]{:S(2)}) copy-start(f32[128,768]{1,0:T(8,128)S(1)} %get-tuple-element.291) | copy-start | bytes 1179652
  343.9 69.9 %reduce-scatter.21.cloned.1.call-start = ((), (), s32[]{:S(2)}) async-start(), calls=%async_computation.15 | async-start | bytes 1769472
  346.6 123.6 %reduce-scatter.23.cloned.1.call-start = ((), (), s32[]{:S(2)}) async-start(), calls=%async_computation.16 | async-start | bytes 4423680
  379.4 39.3 %copy-start.5 = (bf16[768,128]{1,0:T(8,128)(2,1)}, bf16[768,128]{1,0:T(8,128)(2,1)S(1)}, u32[]{:S(2)}) copy-start(bf16[768,128]{1,0:T(8,128)(2,1)S(1)} %copy.41) | copy-start | bytes 589828
  414.9 3.8 copy-start.6
  424.5 0.9 copy-start.8
  424.5 77.9 %reduce-scatter.13.cloned.1.call-start = ((), (), s32[]{:S(2)}) async-start(), calls=%async_computation.11 | async-start | bytes 1474560 | tf_op jit(solution)/shard_map/reduce_scatter | solution.py:226
  426.9 135.4 %reduce-scatter.15.cloned.1.call-start = ((), (), s32[]{:S(2)}) async-start(), calls=%async_computation.12 | async-start | bytes 5898240 | tf_op jit(solution)/shard_map/reduce_scatter | solution.py:238
  430.9 191.4 %reduce-scatter.17.cloned.1.call-start = ((), (), s32[]{:S(2)}) async-start(), calls=%async_computation.13 | async-start | bytes 5898240 | tf_op jit(solution)/shard_map/reduce_scatter | solution.py:244
  434.5 281.7 %all-reduce.23.cloned.1.call-start = ((), (), s32[]{:S(2)}) async-start(), calls=%async_computation.17 | async-start | bytes 7667712 | tf_op jit(solution)/shard_map/psum | solution.py:258
  622.3 6.6 copy-start.18
  622.3 60.8 %copy-start.17 = (f32[128]{0:T(128)S(1)}, f32[128]{0:T(128)}, u32[]{:S(2)}) copy-start(f32[128]{0:T(128)} %copy-done.16) | copy-start | bytes 1540
  622.3 62.6 %copy-start = (bf16[768,2304]{1,0:T(8,128)(2,1)S(1)}, bf16[768,2304]{1,0:T(8,128)(2,1)}, u32[]{:S(2)}) copy-start(bf16[768,2304]{1,0:T(8,128)(2,1)} %all-gather.7.cloned.1.call-done) | copy-start | bytes 10616836
  716.2 3.0 copy-start.11
  719.2 1.7 copy-start.12
  720.8 1.6 copy-start.13
Sparse Core Ops, SparseCore 0:
  9.8 49.9 all-gather.6
  64.1 27.0 all-gather.8
  93.4 25.7 all-gather.10
  121.0 41.8 all-gather.12
  164.6 57.0 all-gather.14
  344.0 34.2 reduce-scatter.18
  381.2 32.5 reduce-scatter.20
  424.7 45.4 reduce-scatter.22
  473.7 28.7 reduce-scatter.12
  505.3 56.9 reduce-scatter.14
  565.3 56.9 reduce-scatter.16
  625.4 90.7 all-reduce.22
